TPU v7x, 32 devices: a whole 2x2x4 slice. The times are simulated.
32 devices in a mesh: groups: 2 (over y), head: 8 (over z, x), blk: 2 (over core).
Axes of the slice: x: 2, y: 2, z: 4, core: 2. Of those that a mesh axis runs over, the one named last changes fastest.
Arguments:
- queries: bfloat16 [256, 4096], P(('groups', 'head', 'blk')), parts along dimension 0, may hold values from -36 to 36
- keys: bfloat16 [256, 4096], P(('groups', 'head', 'blk')), parts along dimension 0, may hold values from -6 to 6
- values: bfloat16 [256, 4096], P(('groups', 'head', 'blk')), parts along dimension 0, may hold values from -12 to 12
- tile_mask: int32 [64, 1, 1], P('groups'), parts along dimension 0, may hold values from 0 to 1, as said below
Outputs:
- attended: bfloat16 [256, 4096], P(('groups', 'head', 'blk')), parts along dimension 0
There are 2 independent parts, one for each index of `groups`. A program takes and returns all parts, laid end to end along the dimension named above; each array names one. Nothing has to cross between parts.
Inputs may be any that keep to these rules, and one draw needn't show every extreme that they name: tile_mask[h, t, t] = 1 for every head h and query tile t.
All inputs are finite; a program needn't handle non-finite values.
Results may differ from a plain program's by a relative error of at most 0.005.
Values may be sent and summed in bfloat16 or wider, within the bound.
No kernel may reach another device: no remote copies, remote signals or barrier semaphores. Data moves between devices by JAX's collectives and lax.ppermute only.
A program may use at most 64 MiB of HBM per device.

v0:
```python
import jax
import jax.numpy as jnp
from jax import lax
from jax.sharding import PartitionSpec as P

H = 32
HD = 128
TILE = 128


big_negative = -1e30


def from_behind(array, axis, by):
    count = lax.axis_size(axis)
    return lax.ppermute(array, axis, [(i, (i + by) % count) for i in range(count)])


def update_block(inputs, k_rows, v_rows, k_tiles, heads_mask, score_scale):
    q_piece, q_tiles, out_sum, row_top, row_total = inputs
    rows_mask = jnp.take(heads_mask, q_tiles, axis=1)
    allowed = jnp.take(rows_mask, k_tiles, axis=2) > 0
    scores = (
        jnp.einsum("qhd,khd->hqk", q_piece, k_rows, preferred_element_type=jnp.float32)
        * score_scale
    )
    scores = jnp.where(allowed, scores, big_negative)
    new_top = jnp.maximum(row_top, jnp.max(scores, axis=2))
    factor = jnp.exp(row_top - new_top)
    weights = jnp.where(allowed, jnp.exp(scores - new_top[:, :, None]), 0.0)
    row_total = row_total * factor + jnp.sum(weights, axis=2)
    out_sum = out_sum * factor[:, :, None] + jnp.einsum(
        "hqk,khd->hqd", weights.astype(jnp.bfloat16), v_rows, preferred_element_type=jnp.float32
    )
    return (out_sum, new_top, row_total)


def attend(q_in, q_index, stacked, key_index_of, pass_on, heads_mask, per_dev, blk_count, my_blk):
    q_rows = q_in.reshape(-1, per_dev, HD)
    row_count = q_rows.shape[0]
    block_count = row_count // row_count
    q_blocks = q_rows.reshape(block_count, row_count, per_dev, HD)
    q_tiles = (q_index // TILE).reshape(block_count, row_count)
    out_sum = jnp.zeros((block_count, per_dev, row_count, HD), jnp.float32)
    row_top = jnp.full((block_count, per_dev, row_count), big_negative, jnp.float32)
    row_total = jnp.zeros((block_count, per_dev, row_count), jnp.float32)
    kv_pair = stacked
    for cycle_step in range(blk_count):
        if cycle_step > 0:
            kv_pair = pass_on(kv_pair)
        k_tiles = key_index_of((my_blk - cycle_step) % blk_count) // TILE
        k_rows = kv_pair[0].reshape(-1, per_dev, HD)
        v_rows = kv_pair[1].reshape(-1, per_dev, HD)

        def step_block(inputs):
            return update_block(inputs, k_rows, v_rows, k_tiles, heads_mask, HD ** (-0.5))

        out_sum, row_top, row_total = lax.map(
            step_block, (q_blocks, q_tiles, out_sum, row_top, row_total)
        )
    out_sum = out_sum.transpose(0, 2, 1, 3).reshape(row_count, per_dev, HD)
    row_top = row_top.transpose(0, 2, 1).reshape(row_count, per_dev)
    row_total = row_total.transpose(0, 2, 1).reshape(row_count, per_dev)
    return (out_sum, row_top, row_total)


def on_device(queries, keys, values, tile_mask):
    head_count = lax.axis_size("head")
    blk_count = lax.axis_size("blk")
    my_head = lax.axis_index("head")
    my_blk = lax.axis_index("blk")
    per_dev = max(1, H // head_count)
    split_count = max(1, head_count // H)
    groups = head_count // split_count
    row_width = per_dev * HD
    query_count = queries.shape[0]
    key_count = keys.shape[0]
    part_id = my_head % split_count
    heads_mask = lax.dynamic_slice_in_dim(tile_mask, my_head // split_count * per_dev, per_dev, 0)
    source = jnp.arange(head_count, dtype=jnp.int32)

    def copy_rows(matrix, row_count):
        shaped = matrix.reshape(row_count, groups, row_width).transpose(1, 0, 2)[:, None]
        return jnp.broadcast_to(shaped, (groups, split_count, row_count, row_width)).reshape(
            head_count, row_count, row_width
        )

    def index_of(per_source, offset, row_count, src_blk):
        starts = (source[:, None] * blk_count + src_blk) * per_source + offset
        return (starts + jnp.arange(row_count, dtype=jnp.int32)[None, :]).reshape(-1)

    sub_rows = query_count // split_count
    shaped = queries.reshape(split_count, query_count // split_count, groups, row_width)
    q_in = lax.all_to_all(
        shaped.transpose(2, 0, 1, 3).reshape(head_count, query_count // split_count, row_width),
        "head",
        split_axis=0,
        concat_axis=0,
        tiled=True,
    )
    k_in, v_in = (
        lax.all_to_all(copy_rows(keys, key_count), "head", split_axis=0, concat_axis=0, tiled=True),
        lax.all_to_all(
            copy_rows(values, key_count), "head", split_axis=0, concat_axis=0, tiled=True
        ),
    )
    kv_stack = jnp.stack([k_in, v_in])

    def pass_on(kv_pair):
        return from_behind(kv_pair, "blk", 1)

    def key_index_of(src_blk):
        return index_of(key_count, 0, key_count, src_blk)

    q_index = index_of(query_count, part_id * sub_rows, sub_rows, my_blk)
    out_sum, row_top, row_total = attend(
        q_in, q_index, kv_stack, key_index_of, pass_on, heads_mask, per_dev, blk_count, my_blk
    )
    result = (
        (out_sum / row_total[:, :, None])
        .astype(jnp.bfloat16)
        .reshape(head_count, sub_rows, row_width)
    )
    returned = lax.all_to_all(result, "head", split_axis=0, concat_axis=0, tiled=True)
    attended = (
        returned.reshape(groups, split_count, sub_rows, row_width)
        .transpose(1, 2, 0, 3)
        .reshape(query_count, H * HD)
    )
    return attended


def solution(mesh):
    in_specs = (
        P(("groups", "head", "blk"), None),
        P(("groups", "head", "blk"), None),
        P(("groups", "head", "blk"), None),
        P("groups", None, None),
    )
    out_specs = P(("groups", "head", "blk"), None)
    return jax.shard_map(
        on_device, mesh=mesh, in_specs=in_specs, out_specs=out_specs, check_vma=False
    )
```

profile of v0, /device:TPU:0, one launch (start us, length us, event | category | flops | bytes accessed | tf_op | source)
XLA Modules:
  0.0 46.3 jit_solution(11785490552753711157)
XLA Ops:
  0.0 0.0 copy-start
  0.0 7.4 %all-to-all-start.1 = ((bf16[8,8,512]{2,1,0:T(8,128)(2,1)}), bf16[8,8,512]{2,1,0:T(8,128)(2,1)S(1)}, u32[]{:S(2)}, u32[]{:S(2)}) async-start(bf16[8,8,512]{2,1,0:T(8,128)(2,1)} %bitcast.59), calls=%async_computation.1 | async-start | bytes 131072 | tf_op jit(solution)/shard_map/all_to_all | solution.py:102
  7.4 0.1 iota_add_fusion.2
  7.5 0.1 add.154
  7.6 0.1 iota_add_fusion.1
  7.7 0.1 add.161
  7.8 0.1 iota_add_fusion
  7.9 0.1 add.169
  8.0 0.0 copy-done
  8.0 0.1 dynamic-slice_bitcast_fusion
  8.0 0.1 select_bitcast_fusion
  8.1 6.2 %all-to-all-done.1 = bf16[8,8,512]{2,1,0:T(8,128)(2,1)S(1)} async-done(((bf16[8,8,512]{2,1,0:T(8,128)(2,1)}), bf16[8,8,512]{2,1,0:T(8,128)(2,1)S(1)}, u32[]{:S(2)}, u32[]{:S(2)}) %all-to-all-start.1) | async-done | bytes 65568 | tf_op jit(solution)/shard_map/all_to_all | solution.py:102
  14.3 3.4 %all-to-all-start.2 = ((bf16[8,8,512]{2,1,0:T(8,128)(2,1)}), bf16[8,8,512]{2,1,0:T(8,128)(2,1)S(1)}, u32[]{:S(2)}, u32[]{:S(2)}) async-start(bf16[8,8,512]{2,1,0:T(8,128)(2,1)} %bitcast.8), calls=%async_computation.2 | async-start | bytes 131072 | tf_op jit(solution)/shard_map/all_to_all | solution.py:103
  17.7 6.8 %all-to-all-done.2 = bf16[8,8,512]{2,1,0:T(8,128)(2,1)S(1)} async-done(((bf16[8,8,512]{2,1,0:T(8,128)(2,1)}), bf16[8,8,512]{2,1,0:T(8,128)(2,1)S(1)}, u32[]{:S(2)}, u32[]{:S(2)}) %all-to-all-start.2) | async-done | bytes 65568 | tf_op jit(solution)/shard_map/all_to_all | solution.py:103
  24.5 3.4 %all-to-all-start = ((bf16[8,8,512]{2,1,0:T(8,128)(2,1)}), bf16[8,8,512]{2,1,0:T(8,128)(2,1)S(1)}, u32[]{:S(2)}, u32[]{:S(2)}) async-start(bf16[8,8,512]{2,1,0:T(8,128)(2,1)} %bitcast.4), calls=%async_computation | async-start | bytes 131072 | tf_op jit(solution)/shard_map/all_to_all | solution.py:94
  27.9 0.1 collective-permute-start
  28.0 6.7 %all-to-all-done = bf16[8,8,512]{2,1,0:T(8,128)(2,1)S(1)} async-done(((bf16[8,8,512]{2,1,0:T(8,128)(2,1)}), bf16[8,8,512]{2,1,0:T(8,128)(2,1)S(1)}, u32[]{:S(2)}, u32[]{:S(2)}) %all-to-all-start) | async-done | bytes 65568 | tf_op jit(solution)/shard_map/all_to_all | solution.py:94
  34.7 0.2 fusion.46
  34.9 0.0 collective-permute-done
  35.0 0.2 fusion.45
  35.2 0.1 fusion.7
  35.4 0.3 fusion.3
  35.6 0.3 fusion
  35.9 0.1 copy.18
  36.0 0.1 reshape.168
  36.1 0.1 copy.19
  36.2 0.1 div.54
  36.3 0.1 div.55
  36.4 9.3 %all_to_all.20 = bf16[8,8,512]{2,1,0:T(8,128)(2,1)S(1)} all-to-all(bf16[8,8,512]{2,1,0:T(8,128)(2,1)S(1)} %divide_convert_fusion), channel_id=1, replica_groups=mesh['groups'=2,'head'=8,'blk'=2] {'head'}, dimensions={0} | all-to-all | bytes 131072 | tf_op jit(solution)/shard_map/all_to_all | solution.py:124
  45.7 0.6 %copy.43 = bf16[8,4096]{1,0:T(8,128)(2,1)} copy(bf16[8,4096]{1,0:T(8,128)(2,1)S(1)} %bitcast.58) | data formatting | bytes 131072
  (16 shorter events, 0.2 us)
Async XLA Ops:
  0.0 8.0 %copy-start = (s32[32,1,1]{0,2,1:T(1,128)S(1)}, s32[32,1,1]{0,2,1:T(1,128)}, u32[]{:S(2)}) copy-start(s32[32,1,1]{0,2,1:T(1,128)} %param.11) | copy-start | bytes 388
  0.0 14.3 %all-to-all-start.1 = ((bf16[8,8,512]{2,1,0:T(8,128)(2,1)}), bf16[8,8,512]{2,1,0:T(8,128)(2,1)S(1)}, u32[]{:S(2)}, u32[]{:S(2)}) async-start(bf16[8,8,512]{2,1,0:T(8,128)(2,1)} %bitcast.59), calls=%async_computation.1 | async-start | bytes 131072 | tf_op jit(solution)/shard_map/all_to_all | solution.py:102
  14.3 10.2 %all-to-all-start.2 = ((bf16[8,8,512]{2,1,0:T(8,128)(2,1)}), bf16[8,8,512]{2,1,0:T(8,128)(2,1)S(1)}, u32[]{:S(2)}, u32[]{:S(2)}) async-start(bf16[8,8,512]{2,1,0:T(8,128)(2,1)} %bitcast.8), calls=%async_computation.2 | async-start | bytes 131072 | tf_op jit(solution)/shard_map/all_to_all | solution.py:103
  24.5 10.2 %all-to-all-start = ((bf16[8,8,512]{2,1,0:T(8,128)(2,1)}), bf16[8,8,512]{2,1,0:T(8,128)(2,1)S(1)}, u32[]{:S(2)}, u32[]{:S(2)}) async-start(bf16[8,8,512]{2,1,0:T(8,128)(2,1)} %bitcast.4), calls=%async_computation | async-start | bytes 131072 | tf_op jit(solution)/shard_map/all_to_all | solution.py:94
  27.9 7.0 %collective-permute-start = (bf16[2,8,8,512]{3,2,1,0:T(8,128)(2,1)S(1)}, bf16[2,8,8,512]{3,2,1,0:T(8,128)(2,1)S(1)}, u32[]{:S(2)}, u32[]{:S(2)}) collective-permute-start(bf16[2,8,8,512]{3,2,1,0:T(8,128)(2,1)S(1)} %pad_maximum_fusion), channel_id=1, source_target_pairs={{0,1},{1,0},{2,3},{3,2},{4,5},{5,4},{6,7},{7,6},{8,9},{9,8},{10,11... | collective-permute-start | bytes 393224 | tf_op jit(solution)/shard_map/ppermute | solution.py:16
where the time goes:
time: 46.8 us; the launch traced here: 46.3 us
  waiting for transfers between devices  19.7 us (42%)
  starting transfers between devices  14.2 us (30%)
  blocking collectives  9.29 us (20%)
  local copies, waits for them, and re-layouts  1.49 us (3%)
  matrix products  0.94 us (2%)
  other arithmetic  0.55 us (1%)
    all_to_all x1, blocking collectives, on_device(): lax.all_to_all(result, 'head', split_axis=0, concat_axis=0, tiled=True)  9.29 us
    all_to_all x1, starting transfers between devices, on_device(): lax.all_to_all(copy_rows(keys, key_count), 'head', split_axis=0, concat_a...  7.41 us
    all_to_all x1, waiting for transfers between devices, on_device(): lax.all_to_all(copy_rows(values, key_count), 'head', split_axis=0, concat...  6.82 us
    all_to_all x1, waiting for transfers between devices, on_device(): lax.all_to_all(shaped.transpose(2, 0, 1, 3).reshape(head_count, query_cou...  6.69 us
    all_to_all x1, waiting for transfers between devices, on_device(): lax.all_to_all(copy_rows(keys, key_count), 'head', split_axis=0, concat_a...  6.19 us
    all_to_all x1, starting transfers between devices, on_device(): lax.all_to_all(copy_rows(values, key_count), 'head', split_axis=0, concat...  3.35 us
    all_to_all x1, starting transfers between devices, on_device(): lax.all_to_all(shaped.transpose(2, 0, 1, 3).reshape(head_count, query_cou...  3.35 us
  transfers between devices with their start and end apart: 4, of which 3 were waited for; matrix products, arithmetic and copies ran while one was open for 2% of the time, Pallas kernels for 0%

commit v1 on v0

--- a/solution.py
+++ b/solution.py
@@ -1,6 +1,10 @@
+import functools
+
 import jax
 import jax.numpy as jnp
 from jax import lax
+from jax.experimental import pallas as pl
+from jax.experimental.pallas import tpu as pltpu
 from jax.sharding import PartitionSpec as P
 
 H = 32
@@ -64,7 +68,7 @@
     return (out_sum, row_top, row_total)
 
 
-def on_device(queries, keys, values, tile_mask):
+def general(queries, keys, values, tile_mask):
     head_count = lax.axis_size("head")
     blk_count = lax.axis_size("blk")
     my_head = lax.axis_index("head")
@@ -130,6 +134,64 @@
     return attended
 
 
+def attend_kernel(mask_ref, got_ref, out_ref, *, row_count, per_dev):
+    first = (lax.axis_index("head") * lax.axis_size("blk") + lax.axis_index("blk")) * per_dev
+    sources = got_ref.shape[0]
+    for head in range(per_dev):
+        allowed = mask_ref[first + head] > 0
+        columns = slice(head * HD, (head + 1) * HD)
+        q, k, v = (
+            got_ref[:, i * row_count : (i + 1) * row_count, columns].reshape(-1, HD)
+            for i in range(3)
+        )
+        scores = lax.dot_general(
+            q, k, (((1,), (1,)), ((), ())), preferred_element_type=jnp.float32
+        )
+        scores = jnp.where(allowed, scores * HD ** (-0.5), big_negative)
+        top = jnp.max(scores, axis=1, keepdims=True)
+        weights = jnp.where(allowed, jnp.exp(scores - top), 0.0)
+        total = jnp.sum(weights, axis=1, keepdims=True)
+        summed = jnp.dot(
+            weights.astype(jnp.bfloat16), v, preferred_element_type=jnp.float32
+        )
+        out_ref[:, :, columns] = (
+            (summed / total).astype(jnp.bfloat16).reshape(sources, row_count, HD)
+        )
+
+
+def one_tile(queries, keys, values, tile_mask):
+    axes = ("head", "blk")
+    count = lax.axis_size(axes)
+    row_count = queries.shape[0]
+    per_dev = H // count
+    width = per_dev * HD
+    packed = jnp.concatenate(
+        [m.reshape(row_count, count, width).transpose(1, 0, 2) for m in (queries, keys, values)],
+        axis=1,
+    )
+    got = lax.all_to_all(packed, axes, split_axis=0, concat_axis=0, tiled=True)
+    result = pl.pallas_call(
+        functools.partial(attend_kernel, row_count=row_count, per_dev=per_dev),
+        out_shape=jax.ShapeDtypeStruct((count, row_count, width), jnp.bfloat16),
+        in_specs=[
+            pl.BlockSpec(memory_space=pltpu.SMEM),
+            pl.BlockSpec(memory_space=pltpu.VMEM),
+        ],
+        out_specs=pl.BlockSpec(memory_space=pltpu.VMEM),
+        compiler_params=pltpu.CompilerParams(vmem_limit_bytes=4 * 1024 * 1024),
+    )(tile_mask.reshape(-1), got)
+    returned = lax.all_to_all(result, axes, split_axis=0, concat_axis=0, tiled=True)
+    return returned.transpose(1, 0, 2).reshape(row_count, H * HD)
+
+
+def on_device(queries, keys, values, tile_mask):
+    count = lax.axis_size("head") * lax.axis_size("blk")
+    same_rows = queries.shape[0] == keys.shape[0]
+    if same_rows and queries.shape[0] * count == TILE and H % count == 0:
+        return one_tile(queries, keys, values, tile_mask)
+    return general(queries, keys, values, tile_mask)
+
+
 def solution(mesh):
     in_specs = (
         P(("groups", "head", "blk"), None),

time: 46.8 us -> 29.2 us (0.62)
  waiting for transfers between devices: 19.7 us -> 0 us
  blocking collectives: 9.29 us -> 25.6 us
  starting transfers between devices: 14.2 us -> 0 us
  Pallas kernels: 0 us -> 1.14 us
  matrix products: 0.94 us -> 0 us
    all_to_all x3 -> x0, waiting for transfers between devices: 19.7 us -> none  [the longest x1 6.82 us: on_device(): lax.all_to_all(copy_rows(values, key_count), 'head', split_axis=0, concat...]
    all_to_all x1 -> x2, blocking collectives: 9.29 us -> 25.6 us  [the longest x1 16.1 us: one_tile(): got = lax.all_to_all(packed, axes, split_axis=0, concat_axis=0, tiled=True)]
    all_to_all x3 -> x0, starting transfers between devices: 14.1 us -> none  [the longest x1 7.41 us: on_device(): lax.all_to_all(copy_rows(keys, key_count), 'head', split_axis=0, concat_a...]
    pallas_call x0 -> x1, Pallas kernels: none -> 1.14 us  [one_tile(): pl.pallas_call(functools.partial(attend_kernel, row_count=row_count, per_...]
    dot_general x4 -> x0, matrix products: 0.94 us -> none  [the longest x2 0.57 us: update_block(): jnp.einsum('hqk,khd->hqd', weights.astype(jnp.bfloat16), v_rows, preferre...]
    concatenate x0 -> x1, other arithmetic: none -> 0.92 us  [one_tile(): jnp.concatenate([m.reshape(row_count, count, width).transpose(1, 0, 2) fo...]
    unnamed x3, local copies, waits for them, and re-layouts: 0.63 us -> 1.28 us
  transfers between devices with their start and end apart: 4 -> 0, of which waited for: 3 -> 0; matrix products, arithmetic and copies ran while one was open for 2% -> 0% of each run, Pallas kernels for 0% -> 0%
where the time goes in v1:
time: 29.2 us; the launch traced here: 29 us
  blocking collectives  25.6 us (88%)
  local copies, waits for them, and re-layouts  1.28 us (4%)
  Pallas kernels  1.14 us (4%)
  other arithmetic  0.92 us (3%)
    all_to_all x1, blocking collectives, one_tile(): got = lax.all_to_all(packed, axes, split_axis=0, concat_axis=0, tiled=True)  16.1 us
    all_to_all x1, blocking collectives, one_tile(): lax.all_to_all(result, axes, split_axis=0, concat_axis=0, tiled=True)  9.48 us
    unnamed x3, local copies, waits for them, and re-layouts  1.28 us
    pallas_call x1, Pallas kernels, one_tile(): pl.pallas_call(functools.partial(attend_kernel, row_count=row_count, per_...  1.14 us
    concatenate x1, other arithmetic, one_tile(): jnp.concatenate([m.reshape(row_count, count, width).transpose(1, 0, 2) fo...  0.92 us

profile of v1, /device:TPU:0, one launch (start us, length us, event | category | flops | bytes accessed | tf_op | source)
XLA Modules:
  0.0 29.0 jit_solution(17765740215514755194)
XLA Ops:
  0.0 0.9 %pad_maximum_fusion = bf16[16,24,256]{2,1,0:T(8,128)(2,1)S(1)} fusion(bf16[16,8,256]{2,1,0:T(8,128)(2,1)} %bitcast.15, bf16[16,8,256]{2,1,0:T(8,128)(2,1)} %bitcast.16, bf16[16,8,256]{2,1,0:T(8,128)(2,1)} %bitcast.17), kind=kLoop, calls=%fused_computation | loop fusion | flops 589824 | bytes 393216 | tf_op jit(solution)/shard_map/concatenate | solution.py:168
  0.9 16.1 %all_to_all.10.got_ref = bf16[16,24,256]{2,1,0:T(8,128)(2,1)S(1)} all-to-all(bf16[16,24,256]{2,1,0:T(8,128)(2,1)S(1)} %pad_maximum_fusion), channel_id=1, replica_groups=mesh['groups'=2,'head'=8,'blk'=2] {'head','blk'}, dimensions={0} | all-to-all | bytes 393216 | tf_op jit(solution)/shard_map/all_to_all | solution.py:172
  17.1 0.0 copy-start
  17.1 0.7 %copy-done = s32[32,1,1]{0,2,1:T(1,128)S(1)} copy-done((s32[32,1,1]{0,2,1:T(1,128)S(1)}, s32[32,1,1]{0,2,1:T(1,128)}, u32[]{:S(2)}) %copy-start) | copy-done | bytes 152
  17.7 1.1 %shard_map.46 = bf16[16,8,256]{2,1,0:T(8,128)(2,1)S(1)} custom-call(s32[32]{0:T(128)S(1)} %bitcast.13, bf16[16,24,256]{2,1,0:T(8,128)(2,1)S(1)} %all_to_all.10.got_ref), custom_call_target="tpu_custom_call" | custom-call | tf_op jit(solution)/shard_map/pallas_call | solution.py:173
  18.9 9.5 %all_to_all.11 = bf16[16,8,256]{2,1,0:T(8,128)(2,1)S(1)} all-to-all(bf16[16,8,256]{2,1,0:T(8,128)(2,1)S(1)} %shard_map.46), channel_id=1, replica_groups=mesh['groups'=2,'head'=8,'blk'=2] {'head','blk'}, dimensions={0} | all-to-all | bytes 131072 | tf_op jit(solution)/shard_map/all_to_all | solution.py:183
  28.3 0.6 %copy.6 = bf16[8,4096]{1,0:T(8,128)(2,1)} copy(bf16[8,4096]{1,0:T(8,128)(2,1)S(1)} %bitcast.14) | data formatting | bytes 131072
Async XLA Ops:
  17.1 0.7 %copy-start = (s32[32,1,1]{0,2,1:T(1,128)S(1)}, s32[32,1,1]{0,2,1:T(1,128)}, u32[]{:S(2)}) copy-start(s32[32,1,1]{0,2,1:T(1,128)} %param.7) | copy-start | bytes 388

commit v2 on v1

--- a/solution.py
+++ b/solution.py
@@ -134,15 +134,17 @@
     return attended
 
 
-def attend_kernel(mask_ref, got_ref, out_ref, *, row_count, per_dev):
+def attend_kernel(allowed_ref, got_ref, out_ref, *, per_dev):
+    sources, rows, _ = got_ref.shape
+    rows = rows // 3
     first = (lax.axis_index("head") * lax.axis_size("blk") + lax.axis_index("blk")) * per_dev
-    sources = got_ref.shape[0]
+    heads = lax.broadcasted_iota(jnp.int32, allowed_ref.shape, 1)
     for head in range(per_dev):
-        allowed = mask_ref[first + head] > 0
+        allowed = jnp.max(jnp.where(heads == first + head, allowed_ref[...], 0), axis=1, keepdims=True) > 0
         columns = slice(head * HD, (head + 1) * HD)
         q, k, v = (
-            got_ref[:, i * row_count : (i + 1) * row_count, columns].reshape(-1, HD)
-            for i in range(3)
+            got_ref[:, part * rows : (part + 1) * rows, columns].reshape(-1, HD)
+            for part in range(3)
         )
         scores = lax.dot_general(
             q, k, (((1,), (1,)), ((), ())), preferred_element_type=jnp.float32
@@ -155,33 +157,34 @@
             weights.astype(jnp.bfloat16), v, preferred_element_type=jnp.float32
         )
         out_ref[:, :, columns] = (
-            (summed / total).astype(jnp.bfloat16).reshape(sources, row_count, HD)
+            (summed / total).astype(jnp.bfloat16).reshape(sources, rows, HD)
         )
 
 
 def one_tile(queries, keys, values, tile_mask):
     axes = ("head", "blk")
     count = lax.axis_size(axes)
-    row_count = queries.shape[0]
+    rows = queries.shape[0]
     per_dev = H // count
     width = per_dev * HD
+    vmem = pl.BlockSpec(memory_space=pltpu.VMEM)
     packed = jnp.concatenate(
-        [m.reshape(row_count, count, width).transpose(1, 0, 2) for m in (queries, keys, values)],
+        [m.reshape(rows, count, width).transpose(1, 0, 2) for m in (queries, keys, values)],
         axis=1,
     )
+    packed, tile_mask = lax.optimization_barrier((packed, tile_mask))
+    allowed = (tile_mask.reshape(1, H) > 0).astype(jnp.int32)
+    packed, allowed = lax.optimization_barrier((packed, allowed))
     got = lax.all_to_all(packed, axes, split_axis=0, concat_axis=0, tiled=True)
     result = pl.pallas_call(
-        functools.partial(attend_kernel, row_count=row_count, per_dev=per_dev),
-        out_shape=jax.ShapeDtypeStruct((count, row_count, width), jnp.bfloat16),
-        in_specs=[
-            pl.BlockSpec(memory_space=pltpu.SMEM),
-            pl.BlockSpec(memory_space=pltpu.VMEM),
-        ],
-        out_specs=pl.BlockSpec(memory_space=pltpu.VMEM),
+        functools.partial(attend_kernel, per_dev=per_dev),
+        out_shape=jax.ShapeDtypeStruct((count, rows, width), jnp.bfloat16),
+        in_specs=[vmem] * 2,
+        out_specs=vmem,
         compiler_params=pltpu.CompilerParams(vmem_limit_bytes=4 * 1024 * 1024),
-    )(tile_mask.reshape(-1), got)
+    )(allowed, got)
     returned = lax.all_to_all(result, axes, split_axis=0, concat_axis=0, tiled=True)
-    return returned.transpose(1, 0, 2).reshape(row_count, H * HD)
+    return returned.transpose(1, 0, 2).reshape(rows, H * HD)
 
 
 def on_device(queries, keys, values, tile_mask):

time: 29.2 us -> 28.1 us (0.962)
  local copies, waits for them, and re-layouts: 1.28 us -> 0.63 us
  Pallas kernels: 1.14 us -> 0.62 us
    unnamed x3, local copies, waits for them, and re-layouts: 1.28 us -> 0.63 us
    pallas_call x1, Pallas kernels: 1.14 us -> 0.62 us  [one_tile(): pl.pallas_call(functools.partial(attend_kernel, per_dev=per_dev), out_sha...]
where the time goes in v2:
time: 28.1 us; the launch traced here: 27.8 us
  blocking collectives  25.6 us (91%)
  other arithmetic  0.93 us (3%)
  local copies, waits for them, and re-layouts  0.63 us (2%)
  Pallas kernels  0.62 us (2%)
    all_to_all x1, blocking collectives, one_tile(): got = lax.all_to_all(packed, axes, split_axis=0, concat_axis=0, tiled=True)  16.1 us
    all_to_all x1, blocking collectives, one_tile(): lax.all_to_all(result, axes, split_axis=0, concat_axis=0, tiled=True)  9.48 us
    concatenate x1, other arithmetic, one_tile(): jnp.concatenate([m.reshape(rows, count, width).transpose(1, 0, 2) for m i...  0.93 us
    unnamed x3, local copies, waits for them, and re-layouts  0.63 us
    pallas_call x1, Pallas kernels, one_tile(): pl.pallas_call(functools.partial(attend_kernel, per_dev=per_dev), out_sha...  0.62 us

profile of v2, /device:TPU:0, one launch (start us, length us, event | category | flops | bytes accessed | tf_op | source)
XLA Modules:
  0.0 27.8 jit_solution(12670152896439376972)
XLA Ops:
  0.0 0.0 copy-start
  0.0 0.9 %pad_maximum_fusion = bf16[16,24,256]{2,1,0:T(8,128)(2,1)S(1)} fusion(bf16[16,8,256]{2,1,0:T(8,128)(2,1)} %bitcast.15, bf16[16,8,256]{2,1,0:T(8,128)(2,1)} %bitcast.16, bf16[16,8,256]{2,1,0:T(8,128)(2,1)} %bitcast.17), kind=kLoop, calls=%fused_computation | loop fusion | flops 589824 | bytes 393216 | tf_op jit(solution)/shard_map/concatenate | solution.py:171
  0.9 0.0 copy-done
  1.0 16.1 %all_to_all.10.got_ref = bf16[16,24,256]{2,1,0:T(8,128)(2,1)S(1)} all-to-all(bf16[16,24,256]{2,1,0:T(8,128)(2,1)S(1)} %pad_maximum_fusion), channel_id=1, replica_groups=mesh['groups'=2,'head'=8,'blk'=2] {'head','blk'}, dimensions={0} | all-to-all | bytes 393216 | tf_op jit(solution)/shard_map/all_to_all | solution.py:178
  17.1 0.6 %shard_map.46 = bf16[16,8,256]{2,1,0:T(8,128)(2,1)S(1)} custom-call(s32[1,32]{1,0:T(1,128)S(1)} %fusion.allowed_ref, bf16[16,24,256]{2,1,0:T(8,128)(2,1)S(1)} %all_to_all.10.got_ref), custom_call_target="tpu_custom_call" | custom-call | tf_op jit(solution)/shard_map/pallas_call | solution.py:179
  17.7 9.5 %all_to_all.11 = bf16[16,8,256]{2,1,0:T(8,128)(2,1)S(1)} all-to-all(bf16[16,8,256]{2,1,0:T(8,128)(2,1)S(1)} %shard_map.46), channel_id=1, replica_groups=mesh['groups'=2,'head'=8,'blk'=2] {'head','blk'}, dimensions={0} | all-to-all | bytes 131072 | tf_op jit(solution)/shard_map/all_to_all | solution.py:186
  27.2 0.6 %copy.6 = bf16[8,4096]{1,0:T(8,128)(2,1)} copy(bf16[8,4096]{1,0:T(8,128)(2,1)S(1)} %bitcast.14) | data formatting | bytes 131072
  (1 shorter events, 0.0 us)
Async XLA Ops:
  0.0 0.9 %copy-start = (s32[32,1,1]{0,2,1:T(1,128)S(1)}, s32[32,1,1]{0,2,1:T(1,128)}, u32[]{:S(2)}) copy-start(s32[32,1,1]{0,2,1:T(1,128)} %param.7) | copy-start | bytes 388

commit v3 on v2

--- a/solution.py
+++ b/solution.py
@@ -134,13 +134,25 @@
     return attended
 
 
+def slot_order(count):
+    quarter = count // 4
+    return [
+        *range(3 * quarter - 1, 2 * quarter - 1, -1),
+        *range(count - 1, 3 * quarter - 1, -1),
+        *range(2 * quarter - 1, -1, -1),
+    ]
+
+
 def attend_kernel(allowed_ref, got_ref, out_ref, *, per_dev):
     sources, rows, _ = got_ref.shape
     rows = rows // 3
-    first = (lax.axis_index("head") * lax.axis_size("blk") + lax.axis_index("blk")) * per_dev
+    me = lax.axis_index("head") * lax.axis_size("blk") + lax.axis_index("blk")
+    slot = sum(jnp.where(me == d, s, 0) for s, d in enumerate(slot_order(sources)))
+    first = slot * per_dev
     heads = lax.broadcasted_iota(jnp.int32, allowed_ref.shape, 1)
     for head in range(per_dev):
-        allowed = jnp.max(jnp.where(heads == first + head, allowed_ref[...], 0), axis=1, keepdims=True) > 0
+        mine = jnp.where(heads == first + head, allowed_ref[...], 0)
+        allowed = jnp.max(mine, axis=1, keepdims=True) > 0
         columns = slice(head * HD, (head + 1) * HD)
         q, k, v = (
             got_ref[:, part * rows : (part + 1) * rows, columns].reshape(-1, HD)
@@ -162,8 +174,7 @@
 
 
 def one_tile(queries, keys, values, tile_mask):
-    axes = ("head", "blk")
-    count = lax.axis_size(axes)
+    count = lax.axis_size(("head", "blk"))
     rows = queries.shape[0]
     per_dev = H // count
     width = per_dev * HD
@@ -175,7 +186,15 @@
     packed, tile_mask = lax.optimization_barrier((packed, tile_mask))
     allowed = (tile_mask.reshape(1, H) > 0).astype(jnp.int32)
     packed, allowed = lax.optimization_barrier((packed, allowed))
-    got = lax.all_to_all(packed, axes, split_axis=0, concat_axis=0, tiled=True)
+    exchange = functools.partial(
+        lax.all_to_all,
+        axis_name=("head", "blk"),
+        split_axis=0,
+        concat_axis=0,
+        axis_index_groups=[slot_order(count)],
+        tiled=True,
+    )
+    got = exchange(packed)
     result = pl.pallas_call(
         functools.partial(attend_kernel, per_dev=per_dev),
         out_shape=jax.ShapeDtypeStruct((count, rows, width), jnp.bfloat16),
@@ -183,14 +202,14 @@
         out_specs=vmem,
         compiler_params=pltpu.CompilerParams(vmem_limit_bytes=4 * 1024 * 1024),
     )(allowed, got)
-    returned = lax.all_to_all(result, axes, split_axis=0, concat_axis=0, tiled=True)
+    returned = exchange(result)
     return returned.transpose(1, 0, 2).reshape(rows, H * HD)
 
 
 def on_device(queries, keys, values, tile_mask):
     count = lax.axis_size("head") * lax.axis_size("blk")
     same_rows = queries.shape[0] == keys.shape[0]
-    if same_rows and queries.shape[0] * count == TILE and H % count == 0:
+    if same_rows and queries.shape[0] * count == TILE and H % count == 0 and count % 4 == 0:
         return one_tile(queries, keys, values, tile_mask)
     return general(queries, keys, values, tile_mask)
 

time: 28.1 us -> 23.2 us (0.83)
  blocking collectives: 25.6 us -> 20.7 us
    all_to_all x2, blocking collectives: 25.6 us -> 20.7 us  [the longest x1 12.1 us: one_tile(): got = exchange(packed)]
where the time goes in v3:
time: 23.2 us; the launch traced here: 23 us
  blocking collectives  20.7 us (89%)
  other arithmetic  0.93 us (4%)
  Pallas kernels  0.64 us (3%)
  local copies, waits for them, and re-layouts  0.63 us (3%)
    all_to_all x1, blocking collectives, one_tile(): got = exchange(packed)  12.1 us
    all_to_all x1, blocking collectives, one_tile(): returned = exchange(result)  8.65 us
    concatenate x1, other arithmetic, one_tile(): jnp.concatenate([m.reshape(rows, count, width).transpose(1, 0, 2) for m i...  0.93 us
    pallas_call x1, Pallas kernels, one_tile(): pl.pallas_call(functools.partial(attend_kernel, per_dev=per_dev), out_sha...  0.64 us
    unnamed x3, local copies, waits for them, and re-layouts  0.63 us

profile of v3, /device:TPU:0, one launch (start us, length us, event | category | flops | bytes accessed | tf_op | source)
XLA Modules:
  0.0 23.0 jit_solution(7745604695441427946)
XLA Ops:
  0.0 0.0 copy-start
  0.0 0.9 %pad_maximum_fusion = bf16[16,24,256]{2,1,0:T(8,128)(2,1)S(1)} fusion(bf16[16,8,256]{2,1,0:T(8,128)(2,1)} %bitcast.15, bf16[16,8,256]{2,1,0:T(8,128)(2,1)} %bitcast.16, bf16[16,8,256]{2,1,0:T(8,128)(2,1)} %bitcast.17), kind=kLoop, calls=%fused_computation | loop fusion | flops 589824 | bytes 393216 | tf_op jit(solution)/shard_map/concatenate | solution.py:182
  0.9 0.0 copy-done
  1.0 12.1 %all_to_all.10.got_ref = bf16[16,24,256]{2,1,0:T(8,128)(2,1)S(1)} all-to-all(bf16[16,24,256]{2,1,0:T(8,128)(2,1)S(1)} %pad_maximum_fusion), channel_id=1, replica_groups={{11,10,9,8,15,14,13,12,7,6,5,4,3,2,1,0},{27,26,25,24,31,30,29,28,23,22,..., dimensions={0} | all-to-all | bytes 393216 | tf_op jit(solution)/shard_map/all_to_all | solution.py:197
  13.1 0.6 %shard_map.46 = bf16[16,8,256]{2,1,0:T(8,128)(2,1)S(1)} custom-call(s32[1,32]{1,0:T(1,128)S(1)} %fusion.allowed_ref, bf16[16,24,256]{2,1,0:T(8,128)(2,1)S(1)} %all_to_all.10.got_ref), custom_call_target="tpu_custom_call" | custom-call | tf_op jit(solution)/shard_map/pallas_call | solution.py:198
  13.7 8.7 %all_to_all.11 = bf16[16,8,256]{2,1,0:T(8,128)(2,1)S(1)} all-to-all(bf16[16,8,256]{2,1,0:T(8,128)(2,1)S(1)} %shard_map.46), channel_id=1, replica_groups={{11,10,9,8,15,14,13,12,7,6,5,4,3,2,1,0},{27,26,25,24,31,30,29,28,23,22,..., dimensions={0} | all-to-all | bytes 131072 | tf_op jit(solution)/shard_map/all_to_all | solution.py:205
  22.4 0.6 %copy.6 = bf16[8,4096]{1,0:T(8,128)(2,1)} copy(bf16[8,4096]{1,0:T(8,128)(2,1)S(1)} %bitcast.14) | data formatting | bytes 131072
  (1 shorter events, 0.0 us)
Async XLA Ops:
  0.0 0.9 %copy-start = (s32[32,1,1]{0,2,1:T(1,128)S(1)}, s32[32,1,1]{0,2,1:T(1,128)}, u32[]{:S(2)}) copy-start(s32[32,1,1]{0,2,1:T(1,128)} %param.7) | copy-start | bytes 388

commit v4 on v3

--- a/solution.py
+++ b/solution.py
@@ -150,26 +150,33 @@
     slot = sum(jnp.where(me == d, s, 0) for s, d in enumerate(slot_order(sources)))
     first = slot * per_dev
     heads = lax.broadcasted_iota(jnp.int32, allowed_ref.shape, 1)
+    def part_of(part, head):
+        columns = slice(head * HD, (head + 1) * HD)
+        return got_ref[:, part * rows : (part + 1) * rows, columns].reshape(-1, HD)
+
+    scores = [
+        lax.dot_general(
+            part_of(0, head), part_of(1, head), (((1,), (1,)), ((), ())),
+            preferred_element_type=jnp.float32,
+        )
+        for head in range(per_dev)
+    ]
+    allowed = [
+        jnp.max(jnp.where(heads == first + head, allowed_ref[...], 0), axis=1, keepdims=True) > 0
+        for head in range(per_dev)
+    ]
+    weights = []
     for head in range(per_dev):
-        mine = jnp.where(heads == first + head, allowed_ref[...], 0)
-        allowed = jnp.max(mine, axis=1, keepdims=True) > 0
-        columns = slice(head * HD, (head + 1) * HD)
-        q, k, v = (
-            got_ref[:, part * rows : (part + 1) * rows, columns].reshape(-1, HD)
-            for part in range(3)
-        )
-        scores = lax.dot_general(
-            q, k, (((1,), (1,)), ((), ())), preferred_element_type=jnp.float32
-        )
-        scores = jnp.where(allowed, scores * HD ** (-0.5), big_negative)
-        top = jnp.max(scores, axis=1, keepdims=True)
-        weights = jnp.where(allowed, jnp.exp(scores - top), 0.0)
-        total = jnp.sum(weights, axis=1, keepdims=True)
+        masked = jnp.where(allowed[head], scores[head], big_negative)
+        top = jnp.max(masked, axis=1, keepdims=True)
+        weights.append(jnp.where(allowed[head], jnp.exp((masked - top) * HD ** (-0.5)), 0.0))
+    for head in range(per_dev):
         summed = jnp.dot(
-            weights.astype(jnp.bfloat16), v, preferred_element_type=jnp.float32
-        )
-        out_ref[:, :, columns] = (
-            (summed / total).astype(jnp.bfloat16).reshape(sources, rows, HD)
+            weights[head].astype(jnp.bfloat16), part_of(2, head), preferred_element_type=jnp.float32
+        )
+        total = jnp.sum(weights[head], axis=1, keepdims=True)
+        out_ref[:, :, head * HD : (head + 1) * HD] = (
+            (summed * (1.0 / total)).astype(jnp.bfloat16).reshape(sources, rows, HD)
         )
 
 

time: 23.2 us -> 23 us (level)
  no operation moved by 1% of the time
where the time goes in v4:
time: 23 us; the launch traced here: 22.8 us
  blocking collectives  20.7 us (90%)
  other arithmetic  0.93 us (4%)
  local copies, waits for them, and re-layouts  0.63 us (3%)
  Pallas kernels  0.42 us (2%)
    all_to_all x1, blocking collectives, one_tile(): got = exchange(packed)  12.1 us
    all_to_all x1, blocking collectives, one_tile(): returned = exchange(result)  8.65 us
    concatenate x1, other arithmetic, one_tile(): jnp.concatenate([m.reshape(rows, count, width).transpose(1, 0, 2) for m i...  0.93 us
    unnamed x3, local copies, waits for them, and re-layouts  0.63 us

profile of v4, /device:TPU:0, one launch (start us, length us, event | category | flops | bytes accessed | tf_op | source)
XLA Modules:
  0.0 22.8 jit_solution(14253104936789589046)
XLA Ops:
  0.0 0.0 copy-start
  0.0 0.9 %pad_maximum_fusion = bf16[16,24,256]{2,1,0:T(8,128)(2,1)S(1)} fusion(bf16[16,8,256]{2,1,0:T(8,128)(2,1)} %bitcast.15, bf16[16,8,256]{2,1,0:T(8,128)(2,1)} %bitcast.16, bf16[16,8,256]{2,1,0:T(8,128)(2,1)} %bitcast.17), kind=kLoop, calls=%fused_computation | loop fusion | flops 589824 | bytes 393216 | tf_op jit(solution)/shard_map/concatenate | solution.py:189
  0.9 0.0 copy-done
  1.0 12.1 %all_to_all.10.got_ref = bf16[16,24,256]{2,1,0:T(8,128)(2,1)S(1)} all-to-all(bf16[16,24,256]{2,1,0:T(8,128)(2,1)S(1)} %pad_maximum_fusion), channel_id=1, replica_groups={{11,10,9,8,15,14,13,12,7,6,5,4,3,2,1,0},{27,26,25,24,31,30,29,28,23,22,..., dimensions={0} | all-to-all | bytes 393216 | tf_op jit(solution)/shard_map/all_to_all | solution.py:204
  13.1 0.4 %shard_map.46 = bf16[16,8,256]{2,1,0:T(8,128)(2,1)S(1)} custom-call(s32[1,32]{1,0:T(1,128)S(1)} %fusion.allowed_ref, bf16[16,24,256]{2,1,0:T(8,128)(2,1)S(1)} %all_to_all.10.got_ref), custom_call_target="tpu_custom_call" | custom-call | tf_op jit(solution)/shard_map/pallas_call | solution.py:205
  13.5 8.7 %all_to_all.11 = bf16[16,8,256]{2,1,0:T(8,128)(2,1)S(1)} all-to-all(bf16[16,8,256]{2,1,0:T(8,128)(2,1)S(1)} %shard_map.46), channel_id=1, replica_groups={{11,10,9,8,15,14,13,12,7,6,5,4,3,2,1,0},{27,26,25,24,31,30,29,28,23,22,..., dimensions={0} | all-to-all | bytes 131072 | tf_op jit(solution)/shard_map/all_to_all | solution.py:212
  22.1 0.6 %copy.6 = bf16[8,4096]{1,0:T(8,128)(2,1)} copy(bf16[8,4096]{1,0:T(8,128)(2,1)S(1)} %bitcast.14) | data formatting | bytes 131072
  (1 shorter events, 0.0 us)
Async XLA Ops:
  0.0 0.9 %copy-start = (s32[32,1,1]{0,2,1:T(1,128)S(1)}, s32[32,1,1]{0,2,1:T(1,128)}, u32[]{:S(2)}) copy-start(s32[32,1,1]{0,2,1:T(1,128)} %param.7) | copy-start | bytes 388

commit v5 on v4

--- a/solution.py
+++ b/solution.py
@@ -134,20 +134,18 @@
     return attended
 
 
-def slot_order(count):
-    quarter = count // 4
-    return [
-        *range(3 * quarter - 1, 2 * quarter - 1, -1),
-        *range(count - 1, 3 * quarter - 1, -1),
-        *range(2 * quarter - 1, -1, -1),
-    ]
+def slot_order():
+    chips, cores = lax.axis_size("head"), lax.axis_size("blk")
+    half = chips // 2
+    order = [*range(half + 1, chips), half, half - 1, *range(half - 1)]
+    return [chip * cores + core for chip in order for core in reversed(range(cores))]
 
 
 def attend_kernel(allowed_ref, got_ref, out_ref, *, per_dev):
     sources, rows, _ = got_ref.shape
     rows = rows // 3
     me = lax.axis_index("head") * lax.axis_size("blk") + lax.axis_index("blk")
-    slot = sum(jnp.where(me == d, s, 0) for s, d in enumerate(slot_order(sources)))
+    slot = sum(jnp.where(me == d, s, 0) for s, d in enumerate(slot_order()))
     first = slot * per_dev
     heads = lax.broadcasted_iota(jnp.int32, allowed_ref.shape, 1)
     def part_of(part, head):
@@ -198,7 +196,7 @@
         axis_name=("head", "blk"),
         split_axis=0,
         concat_axis=0,
-        axis_index_groups=[slot_order(count)],
+        axis_index_groups=[slot_order()],
         tiled=True,
     )
     got = exchange(packed)
@@ -216,7 +214,7 @@
 def on_device(queries, keys, values, tile_mask):
     count = lax.axis_size("head") * lax.axis_size("blk")
     same_rows = queries.shape[0] == keys.shape[0]
-    if same_rows and queries.shape[0] * count == TILE and H % count == 0 and count % 4 == 0:
+    if same_rows and queries.shape[0] * count == TILE and H % count == 0 and lax.axis_size("head") % 2 == 0:
         return one_tile(queries, keys, values, tile_mask)
     return general(queries, keys, values, tile_mask)
 

time: 23 us -> 22.7 us (0.987)
  blocking collectives: 20.7 us -> 20.4 us
    all_to_all x1, blocking collectives: 12.1 us -> 11.8 us  [one_tile(): got = exchange(packed)]
where the time goes in v5:
time: 22.7 us; the launch traced here: 22.5 us
  blocking collectives  20.4 us (90%)
  other arithmetic  0.93 us (4%)
  local copies, waits for them, and re-layouts  0.63 us (3%)
  Pallas kernels  0.42 us (2%)
    all_to_all x1, blocking collectives, one_tile(): got = exchange(packed)  11.8 us
    all_to_all x1, blocking collectives, one_tile(): returned = exchange(result)  8.65 us
    concatenate x1, other arithmetic, one_tile(): jnp.concatenate([m.reshape(rows, count, width).transpose(1, 0, 2) for m i...  0.93 us
    unnamed x3, local copies, waits for them, and re-layouts  0.63 us

profile of v5, /device:TPU:0, one launch (start us, length us, event | category | flops | bytes accessed | tf_op | source)
XLA Modules:
  0.0 22.5 jit_solution(12485775176331337254)
XLA Ops:
  0.0 0.0 copy-start
  0.0 0.9 %pad_maximum_fusion = bf16[16,24,256]{2,1,0:T(8,128)(2,1)S(1)} fusion(bf16[16,8,256]{2,1,0:T(8,128)(2,1)} %bitcast.15, bf16[16,8,256]{2,1,0:T(8,128)(2,1)} %bitcast.16, bf16[16,8,256]{2,1,0:T(8,128)(2,1)} %bitcast.17), kind=kLoop, calls=%fused_computation | loop fusion | flops 589824 | bytes 393216 | tf_op jit(solution)/shard_map/concatenate | solution.py:187
  0.9 0.0 copy-done
  1.0 11.8 %all_to_all.10.got_ref = bf16[16,24,256]{2,1,0:T(8,128)(2,1)S(1)} all-to-all(bf16[16,24,256]{2,1,0:T(8,128)(2,1)S(1)} %pad_maximum_fusion), channel_id=1, replica_groups={{11,10,13,12,15,14,9,8,7,6,1,0,3,2,5,4},{27,26,29,28,31,30,25,24,23,22,..., dimensions={0} | all-to-all | bytes 393216 | tf_op jit(solution)/shard_map/all_to_all | solution.py:202
  12.8 0.4 %shard_map.46 = bf16[16,8,256]{2,1,0:T(8,128)(2,1)S(1)} custom-call(s32[1,32]{1,0:T(1,128)S(1)} %fusion.allowed_ref, bf16[16,24,256]{2,1,0:T(8,128)(2,1)S(1)} %all_to_all.10.got_ref), custom_call_target="tpu_custom_call" | custom-call | tf_op jit(solution)/shard_map/pallas_call | solution.py:203
  13.2 8.6 %all_to_all.11 = bf16[16,8,256]{2,1,0:T(8,128)(2,1)S(1)} all-to-all(bf16[16,8,256]{2,1,0:T(8,128)(2,1)S(1)} %shard_map.46), channel_id=1, replica_groups={{11,10,13,12,15,14,9,8,7,6,1,0,3,2,5,4},{27,26,29,28,31,30,25,24,23,22,..., dimensions={0} | all-to-all | bytes 131072 | tf_op jit(solution)/shard_map/all_to_all | solution.py:210
  21.8 0.6 %copy.6 = bf16[8,4096]{1,0:T(8,128)(2,1)} copy(bf16[8,4096]{1,0:T(8,128)(2,1)S(1)} %bitcast.14) | data formatting | bytes 131072
  (1 shorter events, 0.0 us)
Async XLA Ops:
  0.0 0.9 %copy-start = (s32[32,1,1]{0,2,1:T(1,128)S(1)}, s32[32,1,1]{0,2,1:T(1,128)}, u32[]{:S(2)}) copy-start(s32[32,1,1]{0,2,1:T(1,128)} %param.7) | copy-start | bytes 388
